TPU v7x, 32 devices: a whole 2x2x4 slice. The times are simulated.
32 devices in a mesh: dp: 4 (over z), seq: 8 (over y, x, core).
Axes of the slice: x: 2, y: 2, z: 4, core: 2. Of those that a mesh axis runs over, the one named last changes fastest.
Arguments:
- layer_input: bfloat16 [4, 2048, 1024], P('dp', 'seq'), may hold values from -6 to 6
- w_qkv: bfloat16 [1024, 3072], replicated, may hold values from -8.75 to 8.75
- w_out: bfloat16 [1024, 1024], replicated, may hold values from -0.1875 to 0.1875
- w_proj: bfloat16 [16, 64, 256], replicated, may hold values from -35 to 35
- w_up: bfloat16 [1024, 4096], P('dp', 'seq'), may hold values from -0.1875 to 0.1875
- w_down: bfloat16 [1024, 4096], P('dp', 'seq'), may hold values from -0.09375 to 0.09375
Outputs:
- layer_output: bfloat16 [4, 2048, 1024], P('dp', 'seq')
All inputs are finite; a program needn't handle non-finite values.
Results may differ from a plain program's by a relative error of at most 0.025.
The roundings to bfloat16 on the way count: a program that leaves them out, or rounds other values in their place, can miss the bound.
Values may be sent and summed in bfloat16 or wider, within the bound.
No kernel may reach another device: no remote copies, remote signals or barrier semaphores. Data moves between devices by JAX's collectives and lax.ppermute only.
A program may use at most 128 MiB of HBM per device.

v0:
```python
import jax
import jax.numpy as jnp
from jax import lax
from jax.sharding import PartitionSpec as P

D = 1024
H = 16
HS = 64
WBLK = 256
epsilon = 1e-05


def extended_2(x, sides, width):
    for axis, dim in sides:
        peers, length = (lax.axis_size(axis), x.shape[dim])
        up = [(i, (i + 1) % peers) for i in range(peers - 1)]
        down = [(j, i) for i, j in up]
        last = lax.slice_in_dim(x, length - width, length, axis=dim)
        initial = lax.slice_in_dim(x, 0, width, axis=dim)
        before = lax.ppermute(last, axis, up)
        after = lax.ppermute(initial, axis, down)
        x = jnp.concatenate([before, x, after], axis=dim)
    return x


def normalize(value):
    center = value - jnp.mean(value, axis=-1, keepdims=True)
    spread = jnp.mean(center * center, axis=-1, keepdims=True)
    return center * lax.rsqrt(spread + epsilon)


def attend(block_query, near_keys, near_values, inside, far_keys, far_values):
    scale = HS ** (-0.5)
    near = (
        jnp.einsum("qhd,khd->hqk", block_query, near_keys, preferred_element_type=jnp.float32)
        * scale
    )
    near = jnp.where(inside[None, None, :], near, -jnp.inf)
    far = (
        jnp.einsum("qhd,hrd->hqr", block_query, far_keys, preferred_element_type=jnp.float32)
        * scale
    )
    weights = jax.nn.softmax(jnp.concatenate([near, far], axis=-1), axis=-1).astype(jnp.bfloat16)
    reach = near_keys.shape[0]
    mixed = jnp.einsum(
        "hqk,khd->qhd", weights[..., :reach], near_values, preferred_element_type=jnp.float32
    )
    mixed = mixed + jnp.einsum(
        "hqr,hrd->qhd", weights[..., reach:], far_values, preferred_element_type=jnp.float32
    )
    return mixed.astype(jnp.bfloat16).reshape(block_query.shape[0], H * HS)


def weighted_sums(exponent, paired):
    upper = exponent.astype(jnp.bfloat16)
    lower = (exponent - upper.astype(jnp.float32)).astype(jnp.bfloat16)
    sums = jnp.einsum("hnr,nhc->hrc", upper, paired, preferred_element_type=jnp.float32)
    return sums + jnp.einsum("hnr,nhc->hrc", lower, paired, preferred_element_type=jnp.float32)


def on_device(layer_input, w_qkv, w_out, w_proj, w_up, w_down):
    tokens = layer_input[0]
    rows = tokens.shape[0]
    normed = normalize(tokens.astype(jnp.float32)).astype(jnp.bfloat16)
    qkv = jnp.dot(normed, w_qkv, preferred_element_type=jnp.float32).astype(jnp.bfloat16)
    query = qkv[:, :D].reshape(rows, H, HS)
    keys = qkv[:, D : 2 * D].reshape(rows, H, HS)
    values = qkv[:, 2 * D :].reshape(rows, H, HS)
    paired = jnp.concatenate([keys, values], axis=-1)
    logits = jnp.einsum("nhd,hdr->hnr", keys, w_proj, preferred_element_type=jnp.float32)
    peaks = jnp.max(logits, axis=1)
    peaks = lax.pmax(peaks, "seq")
    exponent = jnp.exp(logits - peaks[:, None, :])
    totals = jnp.sum(exponent, axis=1)
    sums = weighted_sums(exponent, paired)
    totals, sums = (
        lax.psum(totals.astype(jnp.bfloat16), "seq").astype(jnp.float32),
        lax.psum(sums.astype(jnp.bfloat16), "seq").astype(jnp.float32),
    )
    summary = sums / totals[..., None]
    far_keys = normalize(summary[..., :HS]).astype(jnp.bfloat16)
    far_values = normalize(summary[..., HS:]).astype(jnp.bfloat16)
    local_pairs = normalize(paired.astype(jnp.float32).reshape(rows, H, 2, HS)).astype(jnp.bfloat16)
    local_pairs = local_pairs.reshape(rows, 2 * D)
    extended = extended_2(local_pairs, (("seq", 0),), WBLK)
    extended = extended.reshape(rows + 2 * WBLK, H, 2 * HS)
    first_place = lax.axis_index("seq") * rows
    length = rows * lax.axis_size("seq")
    offsets = jnp.arange(3 * WBLK, dtype=jnp.int32) - WBLK

    def per_block(which):
        start = which * WBLK
        places = first_place + start + offsets
        inside = (places >= 0) & (places < length)
        return attend(query, extended[..., :HS], extended[..., HS:], inside, far_keys, far_values)

    attn = lax.map(per_block, jnp.arange(rows // WBLK, dtype=jnp.int32)).reshape(rows, D)
    mixed = (
        tokens.astype(jnp.float32) + jnp.dot(attn, w_out, preferred_element_type=jnp.float32)
    ).astype(jnp.bfloat16)
    normed_two = normalize(mixed.astype(jnp.float32)).astype(jnp.bfloat16)
    up_part, down_part = (
        lax.all_gather(w_up, "dp", axis=0, tiled=True),
        lax.all_gather(w_down, "dp", axis=0, tiled=True),
    )
    hidden = jax.nn.gelu(
        jnp.dot(
            normed_two,
            lax.all_gather(up_part, "seq", axis=1, tiled=True),
            preferred_element_type=jnp.float32,
        )
    ).astype(jnp.bfloat16)
    feed = lax.dot_general(
        hidden,
        lax.all_gather(down_part, "seq", axis=1, tiled=True),
        (((1,), (1,)), ((), ())),
        preferred_element_type=jnp.float32,
    )
    result = (mixed.astype(jnp.float32) + feed).astype(jnp.bfloat16)
    return result[None]


def solution(mesh):
    in_specs = (P("dp", "seq", None), P(), P(), P(), P("dp", "seq"), P("dp", "seq"))
    out_specs = P("dp", "seq", None)
    return jax.shard_map(
        on_device, mesh=mesh, in_specs=in_specs, out_specs=out_specs, check_vma=False
    )
```

profile of v0, /device:TPU:0, one launch (start us, length us, event | category | flops | bytes accessed | tf_op | source)
XLA Modules:
  0.0 214.8 jit_solution(4927498811563739137)
XLA Ops:
  11.4 4.9 %convolution_convert_fusion = bf16[256,3072]{1,0:T(8,128)(2,1)S(1)} fusion(bf16[1024,3072]{1,0:T(8,128)(2,1)} %param.7, bf16[1,256,1024]{2,1,0:T(8,128)(2,1)} %param.6, f32[256]{0:T(256)S(1)} %add_rsqrt_fusion.4, f32[256]{0:T(256)S(1)} %broadcast_multiply_fusion.4), kind=kOutput, calls=%fused_computation.18 | convolution fusion | flops 1612447744 | bytes 8390656 | tf_op jit(solution)/shard_map/dot_general | solution.py:65
  18.8 1.4 copy.25
  20.2 1.3 copy.26
  21.5 3.7 %fusion.88 = (f32[16,256]{1,0:T(8,128)S(1)}, f32[16,256,256]{2,1,0:T(8,128)}) fusion(bf16[256,16,64]{0,2,1:T(8,128)(2,1)S(1)} %bitcast.41, bf16[16,64,256]{2,1,0:T(8,128)(2,1)} %param.9), kind=kOutput, calls=%fused_computation.104 | convolution fusion | flops 135262208 | bytes 5259264 | tf_op jit(solution)/shard_map/nhd,hdr->hnr/dot_general | solution.py:70
  25.3 26.3 %pmax.7 = f32[16,256]{1,0:T(8,128)S(1)} all-reduce(f32[16,256]{1,0:T(8,128)S(1)} %get-tuple-element.36), channel_id=1, replica_groups=mesh['dp'=4,'seq'=8] {'seq'}, use_global_device_ids=true, to_apply=%region_5.0 | all-reduce | flops 4096 | bytes 32768 | tf_op jit(solution)/shard_map/pmax | solution.py:72
  51.6 4.4 %fusion.14 = f32[16,256,128]{2,1,0:T(8,128)S(1)} fusion(f32[16,256,256]{2,1,0:T(8,128)} %get-tuple-element.37, f32[16,256]{1,0:T(8,128)S(1)} %pmax.7, bf16[256,16,64]{2,0,1:T(8,128)(2,1)} %copy.26, bf16[256,16,64]{2,0,1:T(8,128)(2,1)} %copy.25), kind=kOutput, calls=%fused_computation.22 | convolution fusion | flops 272629760 | bytes 7356416 | tf_op jit(solution)/shard_map/hnr,nhc->hrc/dot_general | solution.py:57
  56.3 2.7 %add_convert_fusion = bf16[16,256,128]{2,1,0:T(8,128)(2,1)} fusion(f32[16,256,128]{2,1,0:T(8,128)S(1)} %fusion.14, f32[16,256,256]{2,1,0:T(8,128)S(1)} %copy-done.1, f32[16,256]{1,0:T(8,128)S(1)} %pmax.7, bf16[256,16,64]{2,0,1:T(8,128)(2,1)S(1)} %copy-done.3, bf16[256,16,64]{2,0,1:T(8,128)(2,1)S(1)} %copy-done.2), kind=kOutput, calls=%fused_computation.43 | convolution fusion | flops 276824064 | bytes 8404992 | tf_op jit(solution)/shard_map/hnr,nhc->hrc/dot_general | solution.py:58
  59.8 9.7 %all-gather.5.cloned.1.call-done = bf16[1024,512]{1,0:T(8,128)(2,1)} async-done(((bf16[256,512]{1,0:T(8,128)(2,1)}), bf16[1024,512]{1,0:T(8,128)(2,1)}) %all-gather.5.cloned.1.call-update) | async-done | bytes 1048592 | tf_op jit(solution)/shard_map/all_gather | solution.py:103
  71.6 2.3 %collective-permute-start = (bf16[256,2048]{0,1:T(8,128)(2,1)}, bf16[256,2048]{0,1:T(8,128)(2,1)}, u32[]{:S(2)}, u32[]{:S(2)}) collective-permute-start(bf16[256,2048]{0,1:T(8,128)(2,1)} %bitcast.3), channel_id=1, source_target_pairs={{0,1},{1,2},{2,3},{3,4},{4,5},{5,6},{6,7},{8,9},{9,10},{10,11},{11... | collective-permute-start | bytes 3145736 | tf_op jit(solution)/shard_map/ppermute | solution.py:20
  76.4 3.3 %fusion.12 = bf16[16,256]{1,0:T(8,128)(2,1)S(1)} fusion(f32[16,256,256]{2,1,0:T(8,128)} %get-tuple-element.37, f32[16,256]{1,0:T(8,128)S(1)} %pmax.7), kind=kLoop, calls=%fused_computation.19 | loop fusion | flops 2093056 | bytes 4218880 | tf_op jit(solution)/shard_map/reduce_sum | solution.py:74
  79.7 43.4 %psum.15 = bf16[16,256]{1,0:T(8,128)(2,1)S(1)} all-reduce(bf16[16,256]{1,0:T(8,128)(2,1)S(1)} %fusion.12), channel_id=1, replica_groups=mesh['dp'=4,'seq'=8] {'seq'}, use_global_device_ids=true, to_apply=%region_8.0 | all-reduce | flops 4096 | bytes 16384 | tf_op jit(solution)/shard_map/psum | solution.py:77
  123.2 40.4 %all-reduce.2.cloned.1.call-done = bf16[16,256,128]{2,1,0:T(8,128)(2,1)} async-done(((bf16[16,256,128]{2,1,0:T(8,128)(2,1)}), bf16[16,256,128]{2,1,0:T(8,128)(2,1)}) %all-reduce.2.cloned.1.call-update) | async-done | bytes 1048592 | tf_op jit(solution)/shard_map/psum | solution.py:78
  163.5 1.8 convert_divide_fusion
  165.3 1.7 slice_reduce_fusion
  167.0 2.9 %multiply_reduce_fusion = (f32[16,256]{1,0:T(8,128)S(1)}, f32[16,256]{1,0:T(8,128)S(1)}) fusion(f32[16,256,128]{2,1,0:T(8,128)S(1)} %convert_divide_fusion, f32[16,256]{1,0:T(8,128)S(1)} %broadcast_multiply_fusion.1, f32[16,256]{1,0:T(8,128)S(1)} %broadcast_multiply_fusion.2), kind=kLoop, calls=%fused_computation.39 | loop fusion | flops 1564672 | bytes 2162688 | tf_op jit(solution)/shard_map/reduce_sum | solution.py:28
  170.0 4.3 %fusion.90 = (f32[16,256]{1,0:T(8,128)S(1)}, f32[16,256,256]{2,1,0:T(8,128)S(1)}) fusion(bf16[256,16,64]{0,2,1:T(8,128)(2,1)S(1)} %bitcast.49, f32[16,256,128]{2,1,0:T(8,128)S(1)} %convert_divide_fusion, f32[16,256]{1,0:T(8,128)S(1)} %add_rsqrt_fusion.2, f32[16,256]{1,0:T(8,128)S(1)} %broadcast_multiply_fusion.2), kind=kOutput, calls=%fused_computation.106 | convolution fusion | flops 137097216 | bytes 6864896 | tf_op jit(solution)/shard_map/while/body/eval_jaxpr/qhd,hrd->hqr/dot_general | solution.py:40
  174.4 2.0 pad_maximum_fusion
  176.4 2.0 fusion.89
  178.4 3.7 %fusion.1 = f32[16,256]{1,0:T(8,128)S(1)} fusion(f32[16,256,256]{2,1,0:T(8,128)S(1)} %get-tuple-element.41, f32[16,256,768]{2,1,0:T(8,128)S(1)} %get-tuple-element.39, f32[16,256]{1,0:T(8,128)S(1)} %reduce_max.33), kind=kLoop, calls=%fused_computation.4 | loop fusion | flops 12578816 | bytes 16809984 | tf_op jit(solution)/shard_map/while/body/eval_jaxpr/reduce_sum | solution.py:43
  182.1 3.1 %divide_convert_fusion = bf16[16,256,1024]{2,1,0:T(8,128)(2,1)S(1)} fusion(f32[16,256,256]{2,1,0:T(8,128)S(1)} %get-tuple-element.41, f32[16,256,768]{2,1,0:T(8,128)S(1)} %get-tuple-element.39, f32[16,256]{1,0:T(8,128)S(1)} %fusion.1, f32[16,256]{1,0:T(8,128)S(1)} %reduce_max.33), kind=kLoop, calls=%fused_computation.2 | loop fusion | flops 16777216 | bytes 25198592 | tf_op jit(solution)/shard_map/while/body/eval_jaxpr/convert_element_type | solution.py:43
  185.2 4.1 %fusion.23 = f32[16,64,256]{2,1,0:T(8,128)S(1)} fusion(bf16[16,256,1024]{2,1,0:T(8,128)(2,1)S(1)} %divide_convert_fusion, f32[16,256,128]{2,1,0:T(8,128)S(1)} %convert_divide_fusion, f32[16,256]{1,0:T(8,128)S(1)} %add_rsqrt_fusion.1, f32[16,256]{1,0:T(8,128)S(1)} %broadcast_multiply_fusion.1), kind=kOutput, calls=%fused_computation.32 | convolution fusion | flops 135004160 | bytes 5275648 | tf_op jit(solution)/shard_map/while/body/eval_jaxpr/hqr,hrd->qhd/dot_general | solution.py:48
  189.4 2.1 fusion.45
  192.6 3.6 %all-gather.7.cloned.1.call-done = bf16[1024,4096]{1,0:T(8,128)(2,1)} async-done(((bf16[1024,512]{1,0:T(8,128)(2,1)}), bf16[1024,4096]{1,0:T(8,128)(2,1)}) %all-gather.7.cloned.1.call-update) | async-done | bytes 8388624 | tf_op jit(solution)/shard_map/all_gather | solution.py:109
  196.2 11.5 %fusion.54 = bf16[1,256,1024]{2,1,0:T(8,128)(2,1)} fusion(bf16[1024,4096]{1,0:T(8,128)(2,1)} %all-gather.11.cloned.1.call-done, bf16[256,1024]{1,0:T(8,128)(2,1)S(1)} %get-tuple-element.43, bf16[1024,4096]{1,0:T(8,128)(2,1)} %all-gather.7.cloned.1.call-done, f32[256]{0:T(256)S(1)} %add_rsqrt_fusion.3, f32[256]{0:T(256)S(1)} %broadcast_multiply_fusion.3), kind=kOutput, calls=%fused_computation.67 | convolution fusion | flops 4306239488 | bytes 17827840 | tf_op jit(solution)/shard_map/dot_general | solution.py:113
  (54 shorter events, 13.5 us)
Async XLA Ops:
  7.4 184.1 %copy-start = (bf16[1024,1024]{1,0:T(8,128)(2,1)S(1)}, bf16[1024,1024]{1,0:T(8,128)(2,1)}, u32[]{:S(2)}) copy-start(bf16[1024,1024]{1,0:T(8,128)(2,1)} %param.8) | copy-start | bytes 6291460
  7.4 51.7 %all-gather.9.cloned.1.call-start = ((), (), s32[]{:S(2)}) async-start(), calls=%async_computation.3 | async-start | bytes 1310720 | tf_op jit(solution)/shard_map/all_gather | solution.py:104
  8.1 61.3 %all-gather.5.cloned.1.call-start = ((), (), s32[]{:S(2)}) async-start(), calls=%async_computation.1 | async-start | bytes 1310720 | tf_op jit(solution)/shard_map/all_gather | solution.py:103
  8.8 154.7 %all-reduce.2.cloned.1.call-start = ((), (), s32[]{:S(2)}) async-start(), calls=%async_computation | async-start | bytes 2097152 | tf_op jit(solution)/shard_map/psum | solution.py:78
  51.6 4.4 %copy-start.1 = (f32[16,256,256]{2,1,0:T(8,128)S(1)}, f32[16,256,256]{2,1,0:T(8,128)}, u32[]{:S(2)}) copy-start(f32[16,256,256]{2,1,0:T(8,128)} %get-tuple-element.37) | copy-start | bytes 12582916
  51.6 4.4 %copy-start.2 = (bf16[256,16,64]{2,0,1:T(8,128)(2,1)S(1)}, bf16[256,16,64]{2,0,1:T(8,128)(2,1)}, u32[]{:S(2)}) copy-start(bf16[256,16,64]{2,0,1:T(8,128)(2,1)} %copy.25) | copy-start | bytes 1572868
  51.6 4.7 %copy-start.3 = (bf16[256,16,64]{2,0,1:T(8,128)(2,1)S(1)}, bf16[256,16,64]{2,0,1:T(8,128)(2,1)}, u32[]{:S(2)}) copy-start(bf16[256,16,64]{2,0,1:T(8,128)(2,1)} %copy.26) | copy-start | bytes 1572868
  59.0 133.6 %all-gather.11.cloned.1.call-start = ((), (), s32[]{:S(2)}) async-start(), calls=%async_computation.4 | async-start | bytes 9437184 | tf_op jit(solution)/shard_map/all_gather | solution.py:115
  59.7 136.5 %all-gather.7.cloned.1.call-start = ((), (), s32[]{:S(2)}) async-start(), calls=%async_computation.2 | async-start | bytes 9437184 | tf_op jit(solution)/shard_map/all_gather | solution.py:109
  71.6 102.7 %collective-permute-start = (bf16[256,2048]{0,1:T(8,128)(2,1)}, bf16[256,2048]{0,1:T(8,128)(2,1)}, u32[]{:S(2)}, u32[]{:S(2)}) collective-permute-start(bf16[256,2048]{0,1:T(8,128)(2,1)} %bitcast.3), channel_id=1, source_target_pairs={{0,1},{1,2},{2,3},{3,4},{4,5},{5,6},{6,7},{8,9},{9,10},{10,11},{11... | collective-permute-start | bytes 3145736 | tf_op jit(solution)/shard_map/ppermute | solution.py:20
  73.9 100.5 %collective-permute-start.1 = (bf16[256,2048]{0,1:T(8,128)(2,1)}, bf16[256,2048]{0,1:T(8,128)(2,1)}, u32[]{:S(2)}, u32[]{:S(2)}) collective-permute-start(bf16[256,2048]{0,1:T(8,128)(2,1)} %bitcast.3), channel_id=1, source_target_pairs={{1,0},{2,1},{3,2},{4,3},{5,4},{6,5},{7,6},{9,8},{10,9},{11,10},{12... | collective-permute-start | bytes 3145736 | tf_op jit(solution)/shard_map/ppermute | solution.py:21
  176.4 2.0 copy-start.4
  185.2 4.2 %copy-start.5 = (bf16[768,16,128]{0,2,1:T(8,128)(2,1)S(1)}, bf16[768,16,128]{0,2,1:T(8,128)(2,1)}, u32[]{:S(2)}) copy-start(bf16[768,16,128]{0,2,1:T(8,128)(2,1)} %copy-done.4) | copy-start | bytes 9437188
  189.4 2.1 copy-start.6
Sparse Core Ops, SparseCore 0:
  9.7 30.6 all-gather.8
  42.0 27.3 all-gather.4
  71.3 66.7 all-gather.10
  139.8 56.3 all-gather.6
Sparse Core Ops, SparseCore 1:
  59.1 104.4 all-reduce.1
where the time goes:
time: 215 us
  blocking collectives  69.7 us (32%)
  waiting for transfers between devices  55.8 us (26%)
  matrix products  40.5 us (19%)
  other arithmetic  22.3 us (10%)
  between operations  14.9 us (7%)
  local copies, waits for them, and re-layouts  8 us (4%)
  starting transfers between devices  3.7 us (2%)
    psum x1, blocking collectives, on_device(): lax.psum(totals.astype(jnp.bfloat16), 'seq').astype(jnp.float32)  43.4 us
    psum x1, waiting for transfers between devices, on_device(): lax.psum(sums.astype(jnp.bfloat16), 'seq').astype(jnp.float32)  40.4 us
    pmax x1, blocking collectives, on_device(): peaks = lax.pmax(peaks, 'seq')  26.3 us
    dot_general x1, matrix products, on_device(): lax.dot_general(hidden, lax.all_gather(down_part, 'seq', axis=1, tiled=Tr...  11.5 us
    all_gather x1, waiting for transfers between devices, on_device(): lax.all_gather(w_up, 'dp', axis=0, tiled=True)  9.67 us
    reduce_sum x4, other arithmetic, normalize(): spread = jnp.mean(center * center, axis=-1, keepdims=True)  4.91 us
    dot_general x1, matrix products, on_device(): jnp.dot(normed, w_qkv, preferred_element_type=jnp.float32)  4.86 us
    dot_general x1, matrix products, weighted_sums(): jnp.einsum('hnr,nhc->hrc', upper, paired, preferred_element_type=jnp.floa...  4.35 us
  transfers between devices with their start and end apart: 7, of which 3 were waited for; matrix products, arithmetic and copies ran while one was open for 27% of the time, Pallas kernels for 0%

commit v1 on v0

--- a/solution.py
+++ b/solution.py
@@ -75,7 +75,7 @@
     sums = weighted_sums(exponent, paired)
     totals, sums = (
         lax.psum(totals.astype(jnp.bfloat16), "seq").astype(jnp.float32),
-        lax.psum(sums.astype(jnp.bfloat16), "seq").astype(jnp.float32),
+        jnp.sum(lax.all_gather(sums.astype(jnp.bfloat16), "seq"), axis=0).astype(jnp.float32),
     )
     summary = sums / totals[..., None]
     far_keys = normalize(summary[..., :HS]).astype(jnp.bfloat16)

time: 215 us -> 269 us (1.25)
  waiting for transfers between devices: 55.8 us -> 98.9 us
  other arithmetic: 22.3 us -> 32.7 us
  blocking collectives: 69.7 us -> 65.1 us
  matrix products: 40.5 us -> 45 us
    all_gather x1, waiting for transfers between devices: 3.61 us -> 57.6 us  [on_device(): lax.all_gather(up_part, 'seq', axis=1, tiled=True)]
    psum x1 -> x0, waiting for transfers between devices: 40.4 us -> none  [on_device(): lax.psum(sums.astype(jnp.bfloat16), 'seq').astype(jnp.float32)]
    all_gather x1, waiting for transfers between devices: 0.02 us -> 22.1 us  [on_device(): lax.all_gather(down_part, 'seq', axis=1, tiled=True)]
    all_gather x0 -> x1, waiting for transfers between devices: none -> 7.37 us  [on_device(): lax.all_gather(sums.astype(jnp.bfloat16), 'seq')]
    reduce_sum x0 -> x1, other arithmetic: none -> 6.14 us  [on_device(): jnp.sum(lax.all_gather(sums.astype(jnp.bfloat16), 'seq'), axis=0)]
    psum x1, blocking collectives: 43.4 us -> 38.7 us  [on_device(): lax.psum(totals.astype(jnp.bfloat16), 'seq').astype(jnp.float32)]
    dot_general x1, matrix products: 2.03 us -> 6.51 us  [attend(): jnp.einsum('qhd,khd->hqk', block_query, near_keys, preferred_element_type...]
    reduce_sum x1, other arithmetic: 3.7 us -> 8 us  [attend(): jax.nn.softmax(jnp.concatenate([near, far], axis=-1), axis=-1)]
  transfers between devices with their start and end apart: 7 -> 7, of which waited for: 3 -> 4; matrix products, arithmetic and copies ran while one was open for 27% -> 27% of each run, Pallas kernels for 0% -> 0%
where the time goes in v1:
time: 269 us; the launch traced here: 268 us
  waiting for transfers between devices  98.9 us (37%)
  blocking collectives  65.1 us (24%)
  matrix products  45 us (17%)
  other arithmetic  32.7 us (12%)
  between operations  13.5 us (5%)
  local copies, waits for them, and re-layouts  9.52 us (4%)
  starting transfers between devices  3.72 us (1%)
    all_gather x1, waiting for transfers between devices, on_device(): lax.all_gather(up_part, 'seq', axis=1, tiled=True)  57.6 us
    psum x1, blocking collectives, on_device(): lax.psum(totals.astype(jnp.bfloat16), 'seq').astype(jnp.float32)  38.7 us
    pmax x1, blocking collectives, on_device(): peaks = lax.pmax(peaks, 'seq')  26.3 us
    all_gather x1, waiting for transfers between devices, on_device(): lax.all_gather(down_part, 'seq', axis=1, tiled=True)  22.1 us
    dot_general x1, matrix products, on_device(): lax.dot_general(hidden, lax.all_gather(down_part, 'seq', axis=1, tiled=Tr...  11.5 us
    all_gather x1, waiting for transfers between devices, on_device(): lax.all_gather(w_up, 'dp', axis=0, tiled=True)  9.79 us
    reduce_sum x1, other arithmetic, attend(): jax.nn.softmax(jnp.concatenate([near, far], axis=-1), axis=-1)  8 us
    all_gather x1, waiting for transfers between devices, on_device(): lax.all_gather(sums.astype(jnp.bfloat16), 'seq')  7.37 us
  transfers between devices with their start and end apart: 7, of which 4 were waited for; matrix products, arithmetic and copies ran while one was open for 27% of the time, Pallas kernels for 0%

profile of v1, /device:TPU:0, one launch (start us, length us, event | category | flops | bytes accessed | tf_op | source)
XLA Modules:
  0.0 268.4 jit_solution(6999489025287600214)
XLA Ops:
  10.6 4.9 %convolution_convert_fusion = bf16[256,3072]{1,0:T(8,128)(2,1)S(1)} fusion(bf16[1024,3072]{1,0:T(8,128)(2,1)} %param.7, bf16[1,256,1024]{2,1,0:T(8,128)(2,1)} %param.6, f32[256]{0:T(256)S(1)} %add_rsqrt_fusion.4, f32[256]{0:T(256)S(1)} %broadcast_multiply_fusion.4), kind=kOutput, calls=%fused_computation.18 | convolution fusion | flops 1612447744 | bytes 8390656 | tf_op jit(solution)/shard_map/dot_general | solution.py:65
  20.7 3.7 %fusion.88 = (f32[16,256]{1,0:T(8,128)S(1)}, f32[16,256,256]{2,1,0:T(8,128)}) fusion(bf16[256,16,64]{0,2,1:T(8,128)(2,1)S(1)} %bitcast.44, bf16[16,64,256]{2,1,0:T(8,128)(2,1)} %param.9), kind=kOutput, calls=%fused_computation.104 | convolution fusion | flops 135262208 | bytes 5259264 | tf_op jit(solution)/shard_map/nhd,hdr->hnr/dot_general | solution.py:70
  24.4 26.3 %pmax.7 = f32[16,256]{1,0:T(8,128)S(1)} all-reduce(f32[16,256]{1,0:T(8,128)S(1)} %get-tuple-element.36), channel_id=1, replica_groups=mesh['dp'=4,'seq'=8] {'seq'}, use_global_device_ids=true, to_apply=%region_5.0 | all-reduce | flops 4096 | bytes 32768 | tf_op jit(solution)/shard_map/pmax | solution.py:72
  50.8 4.4 %fusion.14 = f32[16,256,128]{2,1,0:T(8,128)S(1)} fusion(f32[16,256,256]{2,1,0:T(8,128)} %get-tuple-element.37, f32[16,256]{1,0:T(8,128)S(1)} %pmax.7, bf16[256,16,64]{2,0,1:T(8,128)(2,1)} %copy.36, bf16[256,16,64]{2,0,1:T(8,128)(2,1)} %copy.35), kind=kOutput, calls=%fused_computation.22 | convolution fusion | flops 272629760 | bytes 7356416 | tf_op jit(solution)/shard_map/hnr,nhc->hrc/dot_general | solution.py:57
  55.4 2.7 %add_convert_fusion = bf16[16,256,128]{2,1,0:T(8,128)(2,1)} fusion(f32[16,256,128]{2,1,0:T(8,128)S(1)} %fusion.14, f32[16,256,256]{2,1,0:T(8,128)S(1)} %copy-done.1, f32[16,256]{1,0:T(8,128)S(1)} %pmax.7, bf16[256,16,64]{2,0,1:T(8,128)(2,1)S(1)} %copy-done.3, bf16[256,16,64]{2,0,1:T(8,128)(2,1)S(1)} %copy-done.2), kind=kOutput, calls=%fused_computation.43 | convolution fusion | flops 276824064 | bytes 8404992 | tf_op jit(solution)/shard_map/hnr,nhc->hrc/dot_general | solution.py:58
  58.8 9.8 %all-gather.7.cloned.1.call-done = bf16[1024,512]{1,0:T(8,128)(2,1)} async-done(((bf16[256,512]{1,0:T(8,128)(2,1)}), bf16[1024,512]{1,0:T(8,128)(2,1)}) %all-gather.7.cloned.1.call-update) | async-done | bytes 1048592 | tf_op jit(solution)/shard_map/all_gather | solution.py:103
  70.7 2.3 collective-permute-start
  75.5 3.3 %fusion.12 = bf16[16,256]{1,0:T(8,128)(2,1)S(1)} fusion(f32[16,256,256]{2,1,0:T(8,128)} %get-tuple-element.37, f32[16,256]{1,0:T(8,128)S(1)} %pmax.7), kind=kLoop, calls=%fused_computation.19 | loop fusion | flops 2093056 | bytes 4218880 | tf_op jit(solution)/shard_map/reduce_sum | solution.py:74
  78.8 38.7 %psum.7 = bf16[16,256]{1,0:T(8,128)(2,1)S(1)} all-reduce(bf16[16,256]{1,0:T(8,128)(2,1)S(1)} %fusion.12), channel_id=1, replica_groups=mesh['dp'=4,'seq'=8] {'seq'}, use_global_device_ids=true, to_apply=%region_8.0 | all-reduce | flops 4096 | bytes 16384 | tf_op jit(solution)/shard_map/psum | solution.py:77
  117.6 2.0 pad_maximum_fusion
  121.2 6.5 %fusion.89 = (f32[16,256]{1,0:T(8,128)S(1)}, f32[16,256,768]{2,1,0:T(8,128)}) fusion(bf16[256,16,64]{0,2,1:T(8,128)(2,1)S(1)} %bitcast.53, bf16[768,16,128]{0,2,1:T(8,128)(2,1)S(1)} %pad_maximum_fusion, pred[768]{0:T(1024)(128)(4,1)S(1)} %fusion.80), kind=kOutput, calls=%fused_computation.105 | convolution fusion | flops 412086272 | bytes 14697472 | tf_op jit(solution)/shard_map/while/body/eval_jaxpr/qhd,khd->hqk/dot_general | solution.py:35
  127.7 7.4 %all-gather.15.cloned.1.call-done = bf16[128,256,128]{2,1,0:T(8,128)(2,1)} async-done(((bf16[16,256,128]{2,1,0:T(8,128)(2,1)}), bf16[128,256,128]{2,1,0:T(8,128)(2,1)}) %all-gather.15.cloned.1.call-update) | async-done | bytes 8388624 | tf_op jit(solution)/shard_map/all_gather | solution.py:78
  135.1 6.1 %reduce_sum.125 = bf16[16,256,128]{2,1,0:T(8,128)(2,1)} reduce(bf16[8,16,256,128]{3,2,1,0:T(8,128)(2,1)} %bitcast.52, bf16[]{:T(256)} %constant.64.clone.1), dimensions={0}, to_apply=%region_6.0 | reduce | flops 3670016 | bytes 9437186 | tf_op jit(solution)/shard_map/reduce_sum | solution.py:78
  141.2 1.8 convert_divide_fusion
  143.0 1.7 slice_reduce_fusion
  144.8 2.9 %multiply_reduce_fusion = (f32[16,256]{1,0:T(8,128)S(1)}, f32[16,256]{1,0:T(8,128)S(1)}) fusion(f32[16,256,128]{2,1,0:T(8,128)S(1)} %convert_divide_fusion, f32[16,256]{1,0:T(8,128)S(1)} %broadcast_multiply_fusion.1, f32[16,256]{1,0:T(8,128)S(1)} %broadcast_multiply_fusion.2), kind=kLoop, calls=%fused_computation.39 | loop fusion | flops 1564672 | bytes 2162688 | tf_op jit(solution)/shard_map/reduce_sum | solution.py:28
  147.7 4.3 %fusion.90 = (f32[16,256]{1,0:T(8,128)S(1)}, f32[16,256,256]{2,1,0:T(8,128)S(1)}) fusion(bf16[256,16,64]{0,2,1:T(8,128)(2,1)S(1)} %bitcast.54, f32[16,256,128]{2,1,0:T(8,128)S(1)} %convert_divide_fusion, f32[16,256]{1,0:T(8,128)S(1)} %add_rsqrt_fusion.2, f32[16,256]{1,0:T(8,128)S(1)} %broadcast_multiply_fusion.2), kind=kOutput, calls=%fused_computation.106 | convolution fusion | flops 137097216 | bytes 6864896 | tf_op jit(solution)/shard_map/while/body/eval_jaxpr/qhd,hrd->hqr/dot_general | solution.py:40
  152.1 8.0 %fusion.1 = f32[16,256]{1,0:T(8,128)S(1)} fusion(f32[16,256,256]{2,1,0:T(8,128)S(1)} %get-tuple-element.41, f32[16,256,768]{2,1,0:T(8,128)} %get-tuple-element.39, f32[16,256]{1,0:T(8,128)S(1)} %reduce_max.33), kind=kLoop, calls=%fused_computation.4 | loop fusion | flops 12578816 | bytes 16809984 | tf_op jit(solution)/shard_map/while/body/eval_jaxpr/reduce_sum | solution.py:43
  160.2 3.1 %divide_convert_fusion = bf16[16,256,1024]{2,1,0:T(8,128)(2,1)S(1)} fusion(f32[16,256,256]{2,1,0:T(8,128)S(1)} %get-tuple-element.41, f32[16,256,768]{2,1,0:T(8,128)S(1)} %bitcast.42, f32[16,256]{1,0:T(8,128)S(1)} %fusion.1, f32[16,256]{1,0:T(8,128)S(1)} %reduce_max.33), kind=kLoop, calls=%fused_computation.2 | loop fusion | flops 16777216 | bytes 25198592 | tf_op jit(solution)/shard_map/while/body/eval_jaxpr/convert_element_type | solution.py:43
  163.2 4.1 %fusion.23 = f32[16,64,256]{2,1,0:T(8,128)S(1)} fusion(bf16[16,256,1024]{2,1,0:T(8,128)(2,1)S(1)} %divide_convert_fusion, f32[16,256,128]{2,1,0:T(8,128)S(1)} %convert_divide_fusion, f32[16,256]{1,0:T(8,128)S(1)} %add_rsqrt_fusion.1, f32[16,256]{1,0:T(8,128)S(1)} %broadcast_multiply_fusion.1), kind=kOutput, calls=%fused_computation.32 | convolution fusion | flops 135004160 | bytes 5275648 | tf_op jit(solution)/shard_map/while/body/eval_jaxpr/hqr,hrd->qhd/dot_general | solution.py:48
  167.4 2.0 fusion.45
  170.6 22.1 %all-gather.13.cloned.1.call-done = bf16[1024,4096]{1,0:T(8,128)(2,1)} async-done(((bf16[1024,512]{1,0:T(8,128)(2,1)}), bf16[1024,4096]{1,0:T(8,128)(2,1)}) %all-gather.13.cloned.1.call-update) | async-done | bytes 8388624 | tf_op jit(solution)/shard_map/all_gather | solution.py:115
  192.7 57.6 %all-gather.9.cloned.1.call-done = bf16[1024,4096]{1,0:T(8,128)(2,1)} async-done(((bf16[1024,512]{1,0:T(8,128)(2,1)}), bf16[1024,4096]{1,0:T(8,128)(2,1)}) %all-gather.9.cloned.1.call-update) | async-done | bytes 8388624 | tf_op jit(solution)/shard_map/all_gather | solution.py:109
  250.3 11.5 %fusion.54 = bf16[1,256,1024]{2,1,0:T(8,128)(2,1)} fusion(bf16[1024,4096]{1,0:T(8,128)(2,1)} %all-gather.13.cloned.1.call-done, bf16[256,1024]{1,0:T(8,128)(2,1)S(1)} %get-tuple-element.43, bf16[1024,4096]{1,0:T(8,128)(2,1)} %all-gather.9.cloned.1.call-done, f32[256]{0:T(256)S(1)} %add_rsqrt_fusion.3, f32[256]{0:T(256)S(1)} %broadcast_multiply_fusion.3), kind=kOutput, calls=%fused_computation.67 | convolution fusion | flops 4306239488 | bytes 17827840 | tf_op jit(solution)/shard_map/dot_general | solution.py:113
  (62 shorter events, 17.6 us)
Async XLA Ops:
  6.5 162.9 %copy-start = (bf16[1024,1024]{1,0:T(8,128)(2,1)S(1)}, bf16[1024,1024]{1,0:T(8,128)(2,1)}, u32[]{:S(2)}) copy-start(bf16[1024,1024]{1,0:T(8,128)(2,1)} %param.8) | copy-start | bytes 6291460
  6.5 51.7 %all-gather.11.cloned.1.call-start = ((), (), s32[]{:S(2)}) async-start(), calls=%async_computation.2 | async-start | bytes 1310720 | tf_op jit(solution)/shard_map/all_gather | solution.py:104
  7.3 61.3 %all-gather.7.cloned.1.call-start = ((), (), s32[]{:S(2)}) async-start(), calls=%async_computation | async-start | bytes 1310720 | tf_op jit(solution)/shard_map/all_gather | solution.py:103
  8.0 127.1 %all-gather.15.cloned.1.call-start = ((), (), s32[]{:S(2)}) async-start(), calls=%async_computation.4 | async-start | bytes 9437184 | tf_op jit(solution)/shard_map/all_gather | solution.py:78
  50.8 4.4 %copy-start.1 = (f32[16,256,256]{2,1,0:T(8,128)S(1)}, f32[16,256,256]{2,1,0:T(8,128)}, u32[]{:S(2)}) copy-start(f32[16,256,256]{2,1,0:T(8,128)} %get-tuple-element.37) | copy-start | bytes 12582916
  50.8 4.4 %copy-start.2 = (bf16[256,16,64]{2,0,1:T(8,128)(2,1)S(1)}, bf16[256,16,64]{2,0,1:T(8,128)(2,1)}, u32[]{:S(2)}) copy-start(bf16[256,16,64]{2,0,1:T(8,128)(2,1)} %copy.35) | copy-start | bytes 1572868
  50.8 4.7 %copy-start.3 = (bf16[256,16,64]{2,0,1:T(8,128)(2,1)S(1)}, bf16[256,16,64]{2,0,1:T(8,128)(2,1)}, u32[]{:S(2)}) copy-start(bf16[256,16,64]{2,0,1:T(8,128)(2,1)} %copy.36) | copy-start | bytes 1572868
  58.2 134.5 %all-gather.13.cloned.1.call-start = ((), (), s32[]{:S(2)}) async-start(), calls=%async_computation.3 | async-start | bytes 9437184 | tf_op jit(solution)/shard_map/all_gather | solution.py:115
  58.8 191.6 %all-gather.9.cloned.1.call-start = ((), (), s32[]{:S(2)}) async-start(), calls=%async_computation.1 | async-start | bytes 9437184 | tf_op jit(solution)/shard_map/all_gather | solution.py:109
  70.7 46.9 %collective-permute-start = (bf16[256,2048]{0,1:T(8,128)(2,1)}, bf16[256,2048]{0,1:T(8,128)(2,1)}, u32[]{:S(2)}, u32[]{:S(2)}) collective-permute-start(bf16[256,2048]{0,1:T(8,128)(2,1)} %bitcast.3), channel_id=1, source_target_pairs={{0,1},{1,2},{2,3},{3,4},{4,5},{5,6},{6,7},{8,9},{9,10},{10,11},{11... | collective-permute-start | bytes 3145736 | tf_op jit(solution)/shard_map/ppermute | solution.py:20
  73.0 44.6 %collective-permute-start.1 = (bf16[256,2048]{0,1:T(8,128)(2,1)}, bf16[256,2048]{0,1:T(8,128)(2,1)}, u32[]{:S(2)}, u32[]{:S(2)}) collective-permute-start(bf16[256,2048]{0,1:T(8,128)(2,1)} %bitcast.3), channel_id=1, source_target_pairs={{1,0},{2,1},{3,2},{4,3},{5,4},{6,5},{7,6},{9,8},{10,9},{11,10},{12... | collective-permute-start | bytes 3145736 | tf_op jit(solution)/shard_map/ppermute | solution.py:21
  119.6 1.6 copy-start.4
  147.7 12.4 %slice-start = ((s8[12582912]{0:T(1024)(128)(4,1)}), s8[4194304]{0:T(1024)(128)(4,1)S(1)}, s32[]{:S(2)}) async-start(s8[12582912]{0:T(1024)(128)(4,1)} %bitcast.41), calls=%async_computation.5 | async-start | bytes 8388608
  152.1 8.0 %slice-start.1 = ((s8[12582912]{0:T(1024)(128)(4,1)}), s8[4194304]{0:T(1024)(128)(4,1)S(1)}, s32[]{:S(2)}) async-start(s8[12582912]{0:T(1024)(128)(4,1)} %bitcast.41), calls=%async_computation.6 | async-start | bytes 8388608
  152.1 8.0 %slice-start.2 = ((s8[12582912]{0:T(1024)(128)(4,1)}), s8[4194304]{0:T(1024)(128)(4,1)S(1)}, s32[]{:S(2)}) async-start(s8[12582912]{0:T(1024)(128)(4,1)} %bitcast.41), calls=%async_computation.7 | async-start | bytes 8388608
  163.2 4.2 %copy-start.5 = (bf16[768,16,128]{0,2,1:T(8,128)(2,1)S(1)}, bf16[768,16,128]{0,2,1:T(8,128)(2,1)}, u32[]{:S(2)}) copy-start(bf16[768,16,128]{0,2,1:T(8,128)(2,1)} %copy-done.4) | copy-start | bytes 9437188
  167.4 2.0 copy-start.6
Sparse Core Ops, SparseCore 0:
  8.9 30.6 all-gather.10
  41.2 27.3 all-gather.6
  70.5 64.5 all-gather.14
  136.8 55.8 all-gather.12
  194.4 55.8 all-gather.8
